TPU v7x, 256 devices: a whole 4x4x8 slice. The times are simulated.
256 devices in a mesh: row: 16 (over y_hi, z), col: 8 (over x, core), rhs: 2 (over y_lo).
Axes of the slice: x: 4, y: 4 (y_hi: 2, y_lo: 2; y = y_hi * 2 + y_lo), z: 8, core: 2. Of those that a mesh axis runs over, the one named last changes fastest.
Arguments:
- lower: float32 [6, 2048, 4, 2048], P(None, 'row', None, 'col'), may hold values from -0.0625 to 0.0625
- inverse: float32 [4, 2048, 2048], P(None, ('col', 'rhs'), 'row'), may hold values from -0.125 to 0.125
- right_side: float32 [6, 2048, 2048], P(None, 'row', 'rhs'), may hold values from -6 to 6
Outputs:
- solved: float32 [4, 2048, 2048], P(None, 'col', 'rhs')
- trailing: float32 [2, 2048, 2048], P(None, 'row', 'rhs')
All inputs are finite; a program needn't handle non-finite values.
Results may differ from a plain program's by a relative error of at most 0.0001.
Values sent between devices are 32-bit elements; how exact they have to be, the bound alone decides.
No kernel may reach another device: no remote copies, remote signals or barrier semaphores. Data moves between devices by JAX's collectives and lax.ppermute only.
A program may use at most 64 MiB of HBM per device.

v0:
```python
import jax
import jax.numpy as jnp
from jax import lax
from jax.sharding import PartitionSpec as P


def apply_block(lower, unknowns, k):
    return jnp.einsum(
        "inc,cr->inr", lower[k + 1 :, :, k, :], unknowns, precision=lax.Precision.HIGHEST
    )


def solve_block(inverse, residual_block, k):
    inverse_rows = lax.all_gather(inverse[k], "rhs", axis=0, tiled=True)
    partial_value = jnp.dot(
        inverse_rows,
        residual_block,
        precision=lax.Precision.HIGHEST,
        preferred_element_type=jnp.float32,
    )
    return lax.psum(partial_value, "row")


def on_device(lower, inverse, right_side):
    chain_len = inverse.shape[0]
    solved_list = []
    current = right_side
    for k in range(chain_len):
        unknowns = solve_block(inverse, current[k], k)
        solved_list.append(unknowns)
        summed = lax.psum(apply_block(lower, unknowns, k), "col")
        current = jnp.concatenate([current[: k + 1], current[k + 1 :] - summed], axis=0)
    trailing = current[chain_len:]
    return (jnp.stack(solved_list), trailing)


def solution(mesh):
    placed = (P(None, "row", None, "col"), P(None, ("col", "rhs"), "row"), P(None, "row", "rhs"))
    return jax.shard_map(
        on_device,
        mesh=mesh,
        in_specs=placed,
        out_specs=(P(None, "col", "rhs"), P(None, "row", "rhs")),
        check_vma=False,
    )
```

profile of v0, /device:TPU:8, one launch (start us, length us, event | category | flops | bytes accessed | tf_op | source)
XLA Modules:
  0.0 973.4 jit_solution(6360658621553922762)
XLA Ops:
  8.2 5.1 all-gather
  13.2 3.0 fusion.4
  16.3 2.2 slice.51
  18.5 158.9 %all-reduce.9.cloned.1.call-done = f32[256,1024]{1,0:T(8,128)} async-done(((f32[256,1024]{1,0:T(8,128)}), f32[256,1024]{1,0:T(8,128)}) %all-reduce.9.cloned.1.call-update) | async-done | bytes 1048592 | tf_op jit(solution)/shard_map/psum | solution.py:21
  177.4 7.8 convolution_bitcast_fusion
  187.0 2.1 copy.29
  189.1 4.9 all-gather.1
  194.0 62.1 %all-reduce.11.cloned.1.call-done = f32[5,128,1024]{1,2,0:T(8,128)} async-done(((f32[5,128,1024]{1,2,0:T(8,128)}), f32[5,128,1024]{1,2,0:T(8,128)}) %all-reduce.11.cloned.1.call-update) | async-done | bytes 2621456 | tf_op jit(solution)/shard_map/psum | solution.py:31
  256.1 2.8 sub.12
  258.9 2.0 convolution_bitcast_fusion.6
  261.1 2.1 slice.55
  263.3 155.9 %all-reduce.13.cloned.1.call-done = f32[256,1024]{1,0:T(8,128)} async-done(((f32[256,1024]{1,0:T(8,128)}), f32[256,1024]{1,0:T(8,128)}) %all-reduce.13.cloned.1.call-update) | async-done | bytes 1048592 | tf_op jit(solution)/shard_map/psum | solution.py:21
  419.1 6.0 convolution_bitcast_fusion.1
  425.2 4.9 all-gather.2
  430.1 64.3 %all-reduce.15.cloned.1.call-done = f32[4,128,1024]{1,2,0:T(8,128)} async-done(((f32[4,128,1024]{1,2,0:T(8,128)}), f32[4,128,1024]{1,2,0:T(8,128)}) %all-reduce.15.cloned.1.call-update) | async-done | bytes 2097168 | tf_op jit(solution)/shard_map/psum | solution.py:31
  501.5 156.2 %all-reduce.17.cloned.1.call-done = f32[256,1024]{1,0:T(8,128)} async-done(((f32[256,1024]{1,0:T(8,128)}), f32[256,1024]{1,0:T(8,128)}) %all-reduce.17.cloned.1.call-update) | async-done | bytes 1048592 | tf_op jit(solution)/shard_map/psum | solution.py:21
  657.7 5.8 convolution_bitcast_fusion.2
  663.6 4.9 all-gather.3
  668.6 62.6 %all-reduce.19.cloned.1.call-done = f32[3,128,1024]{1,2,0:T(8,128)} async-done(((f32[3,128,1024]{1,2,0:T(8,128)}), f32[3,128,1024]{1,2,0:T(8,128)}) %all-reduce.19.cloned.1.call-update) | async-done | bytes 1572880 | tf_op jit(solution)/shard_map/psum | solution.py:31
  733.9 2.0 convolution_bitcast_fusion.4
  737.7 156.1 %all-reduce.21.cloned.1.call-done = f32[256,1024]{1,0:T(8,128)} async-done(((f32[256,1024]{1,0:T(8,128)}), f32[256,1024]{1,0:T(8,128)}) %all-reduce.21.cloned.1.call-update) | async-done | bytes 1048592 | tf_op jit(solution)/shard_map/psum | solution.py:21
  893.8 4.0 convolution_bitcast_fusion.3
  897.9 4.5 pad_maximum_fusion
  902.4 61.6 %all-reduce.23.cloned.1.call-done = f32[2,128,1024]{1,2,0:T(8,128)} async-done(((f32[2,128,1024]{1,2,0:T(8,128)}), f32[2,128,1024]{1,2,0:T(8,128)}) %all-reduce.23.cloned.1.call-update) | async-done | bytes 1048592 | tf_op jit(solution)/shard_map/psum | solution.py:31
  (36 shorter events, 17.4 us)
Async XLA Ops:
  7.2 170.2 %all-reduce.9.cloned.1.call-start = ((), (), s32[]{:S(2)}) async-start(), calls=%async_computation | async-start | bytes 2097152 | tf_op jit(solution)/shard_map/psum | solution.py:21
  16.2 239.9 %all-reduce.11.cloned.1.call-start = ((), (), s32[]{:S(2)}) async-start(), calls=%async_computation.1 | async-start | bytes 5242880 | tf_op jit(solution)/shard_map/psum | solution.py:31
  185.2 1.7 slice-start
  185.2 233.9 %all-reduce.13.cloned.1.call-start = ((), (), s32[]{:S(2)}) async-start(), calls=%async_computation.2 | async-start | bytes 2097152 | tf_op jit(solution)/shard_map/psum | solution.py:21
  260.9 233.5 %all-reduce.15.cloned.1.call-start = ((), (), s32[]{:S(2)}) async-start(), calls=%async_computation.3 | async-start | bytes 4194304 | tf_op jit(solution)/shard_map/psum | solution.py:31
  425.1 232.6 %all-reduce.17.cloned.1.call-start = ((), (), s32[]{:S(2)}) async-start(), calls=%async_computation.4 | async-start | bytes 2097152 | tf_op jit(solution)/shard_map/psum | solution.py:21
  496.2 1.3 copy-start
  499.5 231.7 %copy-start.1 = (f32[4,128,1024]{1,2,0:T(8,128)S(1)}, f32[4,128,1024]{1,2,0:T(8,128)}, u32[]{:S(2)}) copy-start(f32[4,128,1024]{1,2,0:T(8,128)} %copy-done) | copy-start | bytes 6291460
  499.5 231.7 %all-reduce.19.cloned.1.call-start = ((), (), s32[]{:S(2)}) async-start(), calls=%async_computation.5 | async-start | bytes 3145728 | tf_op jit(solution)/shard_map/psum | solution.py:31
  663.6 230.2 %all-reduce.21.cloned.1.call-start = ((), (), s32[]{:S(2)}) async-start(), calls=%async_computation.6 | async-start | bytes 2097152 | tf_op jit(solution)/shard_map/psum | solution.py:21
  732.8 1.2 copy-start.2
  735.9 162.0 %copy-start.4 = (f32[256,1024]{1,0:T(8,128)S(1)}, f32[256,1024]{1,0:T(8,128)}, u32[]{:S(2)}) copy-start(f32[256,1024]{1,0:T(8,128)} %all-reduce.13.cloned.1.call-done) | copy-start | bytes 3145732
  735.9 228.0 %all-reduce.23.cloned.1.call-start = ((), (), s32[]{:S(2)}) async-start(), calls=%async_computation.7 | async-start | bytes 2097152 | tf_op jit(solution)/shard_map/psum | solution.py:31
  897.9 66.1 %copy-start.3 = (f32[3,128,1024]{1,2,0:T(8,128)S(1)}, f32[3,128,1024]{1,2,0:T(8,128)}, u32[]{:S(2)}) copy-start(f32[3,128,1024]{1,2,0:T(8,128)} %copy-done.2) | copy-start | bytes 4718596
Sparse Core Ops, SparseCore 0:
  16.4 161.0 all-reduce.8
  185.4 70.7 all-reduce.10
  261.0 158.0 all-reduce.12
  425.3 69.0 all-reduce.14
  499.6 158.0 all-reduce.16
  663.7 67.4 all-reduce.18
  736.0 157.7 all-reduce.20
  898.0 65.9 all-reduce.22
where the time goes:
time: 974 us; the launch traced here: 973 us
  waiting for transfers between devices  878 us (90%)
  matrix products  32.5 us (3%)
  blocking collectives  19.8 us (2%)
  local copies, waits for them, and re-layouts  16.3 us (2%)
  between operations  14.2 us (1%)
  other arithmetic  12 us (1%)
    psum x4, waiting for transfers between devices, solve_block(): return lax.psum(partial_value, 'row')  627 us
    psum x4, waiting for transfers between devices, on_device(): summed = lax.psum(apply_block(lower, unknowns, k), 'col')  251 us
    dot_general x4, matrix products, apply_block(): jnp.einsum('inc,cr->inr', lower[k + 1:, :, k, :], unknowns, precision=lax...  23.6 us
    all_gather x4, blocking collectives, solve_block(): inverse_rows = lax.all_gather(inverse[k], 'rhs', axis=0, tiled=True)  19.8 us
  transfers between devices with their start and end apart: 8, of which 8 were waited for; matrix products, arithmetic and copies ran while one was open for 1% of the time, Pallas kernels for 0%

commit v1 on v0

--- a/solution.py
+++ b/solution.py
@@ -1,7 +1,15 @@
+import functools
 import jax
 import jax.numpy as jnp
 from jax import lax
 from jax.sharding import PartitionSpec as P
+
+
+def define_frame(arr, peer_axis):
+    return jnp.sum(jax.lax.all_gather(arr, axis_name=peer_axis), 0)
+
+
+loads_store = functools.partial(define_frame, peer_axis="col")
 
 
 def apply_block(lower, unknowns, k):
@@ -28,7 +36,7 @@
     for k in range(chain_len):
         unknowns = solve_block(inverse, current[k], k)
         solved_list.append(unknowns)
-        summed = lax.psum(apply_block(lower, unknowns, k), "col")
+        summed = loads_store(apply_block(lower, unknowns, k))
         current = jnp.concatenate([current[: k + 1], current[k + 1 :] - summed], axis=0)
     trailing = current[chain_len:]
     return (jnp.stack(solved_list), trailing)

time: 974 us -> 1060 us (1.088)
  waiting for transfers between devices: 878 us -> 916 us
  other arithmetic: 12 us -> 41 us
  local copies, waits for them, and re-layouts: 16.3 us -> 34 us
    all_gather x0 -> x4, waiting for transfers between devices: none -> 285 us  [define_frame(): return jnp.sum(jax.lax.all_gather(arr, axis_name=peer_axis), 0)]
    psum x4 -> x0, waiting for transfers between devices: 251 us -> none  [on_device(): summed = lax.psum(apply_block(lower, unknowns, k), 'col')]
    reduce_sum x0 -> x4, other arithmetic: none -> 29.5 us  [define_frame(): return jnp.sum(jax.lax.all_gather(arr, axis_name=peer_axis), 0)]
where the time goes in v1:
time: 1060 us; the launch traced here: 1050 us
  waiting for transfers between devices  916 us (86%)
  other arithmetic  41 us (4%)
  local copies, waits for them, and re-layouts  34 us (3%)
  matrix products  28.9 us (3%)
  blocking collectives  19.8 us (2%)
  between operations  14.3 us (1%)
    psum x4, waiting for transfers between devices, solve_block(): return lax.psum(partial_value, 'row')  630 us
    all_gather x4, waiting for transfers between devices, define_frame(): return jnp.sum(jax.lax.all_gather(arr, axis_name=peer_axis), 0)  285 us
    reduce_sum x4, other arithmetic, define_frame(): return jnp.sum(jax.lax.all_gather(arr, axis_name=peer_axis), 0)  29.5 us
  transfers between devices with their start and end apart: 8, of which 8 were waited for; matrix products, arithmetic and copies ran while one was open for 1% of the time, Pallas kernels for 0%

profile of v1, /device:TPU:8, one launch (start us, length us, event | category | flops | bytes accessed | tf_op | source)
XLA Modules:
  0.0 1054.8 jit_solution(18017311559789292729)
XLA Ops:
  8.2 5.1 all-gather
  13.2 3.0 fusion.4
  18.5 158.9 %all-reduce.5.cloned.1.call-done = f32[256,1024]{1,0:T(8,128)} async-done(((f32[256,1024]{1,0:T(8,128)}), f32[256,1024]{1,0:T(8,128)}) %all-reduce.5.cloned.1.call-update) | async-done | bytes 1048592 | tf_op jit(solution)/shard_map/psum | solution.py:29
  177.4 6.3 convolution_bitcast_fusion
  189.7 4.9 all-gather.2
  194.6 94.7 %all-gather.13.cloned.1.call-done = f32[40,128,1024]{2,1,0:T(8,128)} async-done(((f32[5,128,1024]{2,1,0:T(8,128)}), f32[40,128,1024]{2,1,0:T(8,128)}) %all-gather.13.cloned.1.call-update) | async-done | bytes 20971536 | tf_op jit(solution)/shard_map/all_gather | solution.py:9
  289.3 8.4 reduce_sum.36
  307.0 157.0 %all-reduce.7.cloned.1.call-done = f32[256,1024]{1,0:T(8,128)} async-done(((f32[256,1024]{1,0:T(8,128)}), f32[256,1024]{1,0:T(8,128)}) %all-reduce.7.cloned.1.call-update) | async-done | bytes 1048592 | tf_op jit(solution)/shard_map/psum | solution.py:29
  464.0 6.0 convolution_bitcast_fusion.1
  470.0 2.9 copy.24
  473.0 4.9 all-gather.4
  477.9 80.9 %all-gather.15.cloned.1.call-done = f32[32,128,1024]{2,1,0:T(8,128)} async-done(((f32[4,128,1024]{2,1,0:T(8,128)}), f32[32,128,1024]{2,1,0:T(8,128)}) %all-gather.15.cloned.1.call-update) | async-done | bytes 16777232 | tf_op jit(solution)/shard_map/all_gather | solution.py:9
  558.8 9.3 reduce_sum.37
  578.2 157.1 %all-reduce.9.cloned.1.call-done = f32[256,1024]{1,0:T(8,128)} async-done(((f32[256,1024]{1,0:T(8,128)}), f32[256,1024]{1,0:T(8,128)}) %all-reduce.9.cloned.1.call-update) | async-done | bytes 1048592 | tf_op jit(solution)/shard_map/psum | solution.py:29
  735.3 4.6 convolution_bitcast_fusion.2
  741.7 4.9 all-gather.6
  746.6 63.2 %all-gather.17.cloned.1.call-done = f32[24,128,1024]{2,1,0:T(8,128)} async-done(((f32[3,128,1024]{2,1,0:T(8,128)}), f32[24,128,1024]{2,1,0:T(8,128)}) %all-gather.17.cloned.1.call-update) | async-done | bytes 12582928 | tf_op jit(solution)/shard_map/all_gather | solution.py:9
  809.9 7.4 reduce_sum.38
  817.3 3.2 copy.50
  826.8 157.4 %all-reduce.11.cloned.1.call-done = f32[256,1024]{1,0:T(8,128)} async-done(((f32[256,1024]{1,0:T(8,128)}), f32[256,1024]{1,0:T(8,128)}) %all-reduce.11.cloned.1.call-update) | async-done | bytes 1048592 | tf_op jit(solution)/shard_map/psum | solution.py:29
  984.2 3.0 convolution_bitcast_fusion.3
  988.6 4.0 pad_maximum_fusion
  992.6 46.6 %all-gather.19.cloned.1.call-done = f32[16,128,1024]{2,1,0:T(8,128)} async-done(((f32[2,128,1024]{2,1,0:T(8,128)}), f32[16,128,1024]{2,1,0:T(8,128)}) %all-gather.19.cloned.1.call-update) | async-done | bytes 8388624 | tf_op jit(solution)/shard_map/all_gather | solution.py:9
  1039.2 4.4 reduce_sum.39
  (50 shorter events, 42.2 us)
Async XLA Ops:
  7.2 170.2 %all-reduce.5.cloned.1.call-start = ((), (), s32[]{:S(2)}) async-start(), calls=%async_computation | async-start | bytes 2097152 | tf_op jit(solution)/shard_map/psum | solution.py:29
  16.2 273.1 %all-gather.13.cloned.1.call-start = ((), (), s32[]{:S(2)}) async-start(), calls=%async_computation.4 | async-start | bytes 23592960 | tf_op jit(solution)/shard_map/all_gather | solution.py:9
  185.9 1.7 slice-start
  185.9 278.1 %all-reduce.7.cloned.1.call-start = ((), (), s32[]{:S(2)}) async-start(), calls=%async_computation.1 | async-start | bytes 2097152 | tf_op jit(solution)/shard_map/psum | solution.py:29
  304.6 254.2 %all-gather.15.cloned.1.call-start = ((), (), s32[]{:S(2)}) async-start(), calls=%async_computation.5 | async-start | bytes 18874368 | tf_op jit(solution)/shard_map/all_gather | solution.py:9
  472.9 262.4 %all-reduce.9.cloned.1.call-start = ((), (), s32[]{:S(2)}) async-start(), calls=%async_computation.2 | async-start | bytes 2097152 | tf_op jit(solution)/shard_map/psum | solution.py:29
  572.8 1.3 copy-start
  576.1 233.7 %all-gather.17.cloned.1.call-start = ((), (), s32[]{:S(2)}) async-start(), calls=%async_computation.6 | async-start | bytes 14155776 | tf_op jit(solution)/shard_map/all_gather | solution.py:9
  741.6 242.5 %all-reduce.11.cloned.1.call-start = ((), (), s32[]{:S(2)}) async-start(), calls=%async_computation.3 | async-start | bytes 2097152 | tf_op jit(solution)/shard_map/psum | solution.py:29
  817.3 3.2 copy-start.1
  822.0 1.2 copy-start.2
  825.2 213.9 %all-gather.19.cloned.1.call-start = ((), (), s32[]{:S(2)}) async-start(), calls=%async_computation.7 | async-start | bytes 9437184 | tf_op jit(solution)/shard_map/all_gather | solution.py:9
  826.8 161.8 %copy-start.4 = (f32[256,1024]{1,0:T(8,128)S(1)}, f32[256,1024]{1,0:T(8,128)}, u32[]{:S(2)}) copy-start(f32[256,1024]{1,0:T(8,128)} %all-reduce.7.cloned.1.call-done) | copy-start | bytes 3145732
  826.8 161.8 %copy-start.5 = (f32[256,1024]{1,0:T(8,128)S(1)}, f32[256,1024]{1,0:T(8,128)}, u32[]{:S(2)}) copy-start(f32[256,1024]{1,0:T(8,128)} %all-reduce.9.cloned.1.call-done) | copy-start | bytes 3145732
  1043.6 1.7 copy-start.3
Sparse Core Ops, SparseCore 0:
  16.4 161.0 all-reduce.4
  186.0 103.3 all-gather.12
  304.7 159.2 all-reduce.6
  473.0 85.6 all-gather.14
  576.3 159.0 all-reduce.8
  741.8 68.0 all-gather.16
  825.4 158.7 all-reduce.10
  988.7 50.4 all-gather.18
